TPU v7x, 32 devices: a whole 2x2x4 slice. The times are simulated.
32 devices in a mesh: clip: 8 (over y, x, core), tm: 4 (over z).
Axes of the slice: x: 2, y: 2, z: 4, core: 2. Of those that a mesh axis runs over, the one named last changes fastest.
Arguments:
- features: bfloat16 [16, 4, 64, 1024], P('clip', 'tm'), may hold values from -6 to 6
- flow_forward: int32 [16, 4, 2, 16], P('clip', 'tm'), may hold values from -4 to 4
- flow_backward: int32 [16, 4, 2, 16], P('clip', 'tm'), may hold values from -4 to 4
- w_forward_in: bfloat16 [64, 1152], replicated, may hold values from -0.1875 to 0.1875
- b_forward_in: float32 [64], replicated, may hold values from -3 to 3
- w_forward_out: bfloat16 [64, 576], replicated, may hold values from -0.25 to 0.25
- b_forward_out: float32 [64], replicated, may hold values from -3 to 3
- w_backward_in: bfloat16 [64, 1152], replicated, may hold values from -0.1875 to 0.1875
- b_backward_in: float32 [64], replicated, may hold values from -3 to 3
- w_backward_out: bfloat16 [64, 576], replicated, may hold values from -0.25 to 0.25
- b_backward_out: float32 [64], replicated, may hold values from -3 to 3
- w_merge: bfloat16 [64, 1152], replicated, may hold values from -0.1875 to 0.1875
- b_merge: float32 [64], replicated, may hold values from -3 to 3
- w_head: bfloat16 [48, 64], replicated, may hold values from -0.75 to 0.75
- b_head: float32 [48], replicated, may hold values from -3 to 3
- target: bfloat16 [16, 4, 48, 1024], P('clip', 'tm'), may hold values from -24 to 24
Outputs:
- restored: bfloat16 [16, 4, 48, 1024], P('clip', 'tm')
- grad_merge: float32 [64, 1152], replicated
- grad_head: float32 [48, 64], replicated
- loss: float32 [], replicated
All inputs are finite; a program needn't handle non-finite values.
Results may differ from a plain program's by a relative error of at most 0.0085.
Values may be sent and summed in bfloat16 or wider, within the bound.
A program may use at most 64 MiB of HBM per device.

v0:
```python
import jax
import jax.numpy as jnp
from jax import lax
from jax.sharding import PartitionSpec as P

CHANNELS = 64
SUBPIX = 48
PATCH_ROWS = 32
PATCH_COLS = 32
PIXELS = 1024
flow_reach = 4
tile_rows = 8
block_side = 8
clip_limit = 128.0
leak_slope = 0.1


def shifted(value, axis, steps):
    count = lax.axis_size(axis)
    first, last = (max(0, -steps), min(count, count - steps))
    return lax.ppermute(value, axis, [(source, source + steps) for source in range(first, last)])


def flat_taps(source, height, width):
    pixels = height * width
    padded = jnp.pad(source, ((0, 0), (width + 1, width + 1)))
    col_pos = lax.broadcasted_iota(jnp.int32, (1, pixels), 1) % width
    layers = []
    for row_off in (-1, 0, 1):
        for col_off in (-1, 0, 1):
            start = width + 1 + row_off * width + col_off
            piece = padded[:, start : start + pixels]
            if col_off != 0:
                valid = (col_pos + col_off >= 0) & (col_pos + col_off < width)
                piece = jnp.where(valid, piece, jnp.zeros_like(piece))
            layers.append(piece)
    return layers


def apply_taps(weight, groups):
    total_in = sum((group[0].shape[0] for group in groups))
    result = None
    for tap_index in range(9):
        offset = tap_index * total_in
        for group in groups:
            width_in = group[tap_index].shape[0]
            block = weight[:, offset : offset + width_in]
            term = jnp.dot(block, group[tap_index], preferred_element_type=jnp.float32)
            result = term if result is None else result + term
            offset = offset + width_in
    return result


def warp_state(hidden_state, flow_map, height, width):
    padded = jnp.pad(hidden_state, ((0, 0), (flow_reach * width, flow_reach * width)))
    grid_shape = (height // block_side, width // block_side)
    shift_rows = jnp.repeat(
        jnp.repeat(flow_map[0].reshape(grid_shape), block_side, 0), block_side, 1
    )
    shift_cols = jnp.repeat(
        jnp.repeat(flow_map[1].reshape(grid_shape), block_side, 0), block_side, 1
    )
    row_pos = lax.broadcasted_iota(jnp.int32, (height, width), 0)
    col_pos = lax.broadcasted_iota(jnp.int32, (height, width), 1)
    source_col = col_pos + shift_cols
    inside = (source_col >= 0) & (source_col < width)
    window_rows = tile_rows + 2 * flow_reach
    window_cell = lax.broadcasted_iota(jnp.int32, (window_rows * width, tile_rows * width), 0)
    pieces = []
    for tile_index in range(height // tile_rows):
        row_start = tile_index * tile_rows
        window = padded[:, row_start * width : (row_start + window_rows) * width]
        local_row = (
            row_pos[row_start : row_start + tile_rows]
            + shift_rows[row_start : row_start + tile_rows]
            - row_start
            + flow_reach
        )
        target_cell = local_row * width + source_col[row_start : row_start + tile_rows]
        target_cell = jnp.where(inside[row_start : row_start + tile_rows], target_cell, -1).reshape(
            -1
        )
        one_hot = (window_cell == target_cell[None, :]).astype(jnp.bfloat16)
        pieces.append(jnp.dot(window, one_hot, preferred_element_type=jnp.float32))
    return jnp.concatenate(pieces, axis=1).astype(jnp.bfloat16)


def propagate(prior_state, feature, flow_map, weights, height, width):
    w_first, b_first, w_second, b_second = weights
    warped = warp_state(prior_state, flow_map, height, width)
    first_out = (
        apply_taps(w_first, (flat_taps(warped, height, width), flat_taps(feature, height, width)))
        + b_first[:, None]
    )
    first_out = jax.nn.leaky_relu(first_out, leak_slope).astype(jnp.bfloat16)
    second_out = apply_taps(w_second, (flat_taps(first_out, height, width),)) + b_second[:, None]
    return (warped.astype(jnp.float32) + second_out).astype(jnp.bfloat16)


def merge_and_grade(fwd_state, bwd_state, target_frame, merge_weights, height, width, loss_scale):
    w_merge, b_merge, w_head, b_head = merge_weights
    groups = (flat_taps(fwd_state, height, width), flat_taps(bwd_state, height, width))
    mixed_pre = apply_taps(w_merge, groups) + b_merge[:, None]
    sigmoid_part = jax.nn.sigmoid(mixed_pre)
    active = (mixed_pre * sigmoid_part).astype(jnp.bfloat16)
    output = jnp.dot(w_head, active, preferred_element_type=jnp.float32) + b_head[:, None]
    misfit = output - target_frame.astype(jnp.float32)
    loss_part = 0.5 * loss_scale * jnp.sum(misfit * misfit)
    errors = (misfit * loss_scale).astype(jnp.bfloat16)
    grad_head = lax.dot_general(
        errors, active, (((1,), (1,)), ((), ())), preferred_element_type=jnp.float32
    )
    back_grad = lax.dot_general(
        w_head, errors, (((0,), (0,)), ((), ())), preferred_element_type=jnp.float32
    )
    silu_slope = sigmoid_part * (1.0 + mixed_pre * (1.0 - sigmoid_part))
    d_mixed = (back_grad * silu_slope).astype(jnp.bfloat16)
    blocks = []
    for tap_index in range(9):
        for group in groups:
            blocks.append(
                lax.dot_general(
                    d_mixed,
                    group[tap_index],
                    (((1,), (1,)), ((), ())),
                    preferred_element_type=jnp.float32,
                )
            )
    grad_merge = jnp.concatenate(blocks, axis=1)
    return (output.astype(jnp.bfloat16), grad_merge, grad_head, loss_part)


def on_device(
    features,
    flow_forward,
    flow_backward,
    w_forward_in,
    b_forward_in,
    w_forward_out,
    b_forward_out,
    w_backward_in,
    b_backward_in,
    w_backward_out,
    b_backward_out,
    w_merge,
    b_merge,
    w_head,
    b_head,
    target,
):
    fwd_weights = (w_forward_in, b_forward_in, w_forward_out, b_forward_out)
    bwd_weights = (w_backward_in, b_backward_in, w_backward_out, b_backward_out)
    merge_weights = (w_merge, b_merge, w_head, b_head)
    micro_clips = features.shape[0]
    sections = lax.axis_size("tm")
    section_index = lax.axis_index("tm")
    turns = micro_clips + sections - 1
    frame_feats = features[:, 0]
    fwd_flows = flow_forward[:, 0]
    bwd_flows = flow_backward[:, 0]
    blank_states = jnp.zeros((micro_clips, CHANNELS, PIXELS), jnp.bfloat16)
    seed_state = jnp.zeros((CHANNELS, PIXELS), jnp.bfloat16)
    bwd_offset = sections - 1 - section_index

    def advance(turn_index, offset, incoming, states, flows, weights):
        member = turn_index - offset
        active_flag = (member >= 0) & (member < micro_clips)
        member = jnp.clip(member, 0, micro_clips - 1)
        feature = lax.dynamic_index_in_dim(frame_feats, member, 0, keepdims=False)
        flow_map = lax.dynamic_index_in_dim(flows, member, 0, keepdims=False)
        produced = propagate(incoming, feature, flow_map, weights, PATCH_ROWS, PATCH_COLS)
        former = lax.dynamic_index_in_dim(states, member, 0, keepdims=False)
        states = lax.dynamic_update_index_in_dim(
            states, jnp.where(active_flag, produced, former), member, 0
        )
        return (produced, states)

    def forward_turn(turn_index, carried):
        produced, states = advance(
            turn_index, section_index, carried[0], carried[1], fwd_flows, fwd_weights
        )
        return (shifted(produced, "tm", 1), states)

    def backward_turn(turn_index, carried):
        produced, states = advance(
            turn_index, bwd_offset, carried[0], carried[1], bwd_flows, bwd_weights
        )
        return (shifted(produced, "tm", -1), states)

    fwd_states = lax.fori_loop(0, turns, forward_turn, (seed_state, blank_states))[1]
    bwd_states = lax.fori_loop(0, turns, backward_turn, (seed_state, blank_states))[1]
    loss_scale = 1.0 / (micro_clips * lax.axis_size("clip") * sections)

    def grade_member(totals, inputs):
        frame_out, grad_merge, grad_head, loss_part = merge_and_grade(
            inputs[0], inputs[1], inputs[2], merge_weights, PATCH_ROWS, PATCH_COLS, loss_scale
        )
        return ((totals[0] + grad_merge, totals[1] + grad_head, totals[2] + loss_part), frame_out)

    initial = (
        jnp.zeros((CHANNELS, 18 * CHANNELS), jnp.float32),
        jnp.zeros((SUBPIX, CHANNELS), jnp.float32),
        jnp.zeros((), jnp.float32),
    )
    totals, frames_out = lax.scan(grade_member, initial, (fwd_states, bwd_states, target[:, 0]))
    restored = frames_out[:, None]
    grad_merge, grad_head, loss_total = lax.psum((totals[0], totals[1], totals[2]), ("clip", "tm"))
    squares = jnp.sum(grad_merge * grad_merge) + jnp.sum(grad_head * grad_head)
    factor = jnp.minimum(1.0, clip_limit / jnp.sqrt(squares + 1e-06))
    return (restored, grad_merge * factor, grad_head * factor, loss_total)


def solution(mesh):
    in_specs = (
        P("clip", "tm", None, None),
        P("clip", "tm", None, None),
        P("clip", "tm", None, None),
        P(),
        P(),
        P(),
        P(),
        P(),
        P(),
        P(),
        P(),
        P(),
        P(),
        P(),
        P(),
        P("clip", "tm", None, None),
    )
    out_specs = (P("clip", "tm", None, None), P(), P(), P())
    return jax.shard_map(
        on_device, mesh=mesh, in_specs=in_specs, out_specs=out_specs, check_vma=False
    )
```

profile of v0, /device:TPU:8, one launch (start us, length us, event | category | flops | bytes accessed | tf_op | source)
XLA Modules:
  0.0 339.6 jit_solution(3447712072973825057)
XLA Ops:
  7.4 0.8 copy-done.4
  8.2 85.5 %while.57 = (s32[]{:T(128)}, bf16[64,1024]{1,0:T(8,128)(2,1)S(1)}, bf16[2,64,1024]{2,1,0:T(8,128)(2,1)S(1)}, s32[]{:T(128)}, s32[2,2,16]{2,1,0:T(2,128)S(1)}, /*...) while((s32[]{:T(128)}, bf16[64,1024]{1,0:T(8,128)(2,1)S(1)}, ...), condition=%wide.region_1.2_spmd, body=%wide.region_0.1_spmd.sunk | while | flops 299203584 | bytes 19935880 | solution.py:190
  18.4 3.5 %collective-permute-start = (bf16[64,1024]{1,0:T(8,128)(2,1)S(1)}, bf16[64,1024]{1,0:T(8,128)(2,1)S(1)}, u32[]{:S(2)}, u32[]{:S(2)}) collective-permute-start(bf16[64,1024]{1,0:T(8,128)(2,1)S(1)} %get-tuple-element.1151), channel_id=1, source_target_pairs={{0,1},{1,2},{2,3},{4,5},{5,6},{6,7},{8,9},{9,10},{10,11},{12,13},{... | collective-permute-start | bytes 393224 | tf_op jit(solution)/shard_map/while/body/eval_jaxpr/ppermute | solution.py:21
  21.9 3.6 %collective-permute-done = bf16[64,1024]{1,0:T(8,128)(2,1)S(1)} collective-permute-done((bf16[64,1024]{1,0:T(8,128)(2,1)S(1)}, bf16[64,1024]{1,0:T(8,128)(2,1)S(1)}, u32[]{:S(2)}, u32[]{:S(2)}) %collective-permute-start) | collective-permute-done | bytes 131104 | tf_op jit(solution)/shard_map/while/body/eval_jaxpr/ppermute | solution.py:21
  35.7 3.5 %collective-permute-start = (bf16[64,1024]{1,0:T(8,128)(2,1)S(1)}, bf16[64,1024]{1,0:T(8,128)(2,1)S(1)}, u32[]{:S(2)}, u32[]{:S(2)}) collective-permute-start(bf16[64,1024]{1,0:T(8,128)(2,1)S(1)} %get-tuple-element.1151), channel_id=1, source_target_pairs={{0,1},{1,2},{2,3},{4,5},{5,6},{6,7},{8,9},{9,10},{10,11},{12,13},{... | collective-permute-start | bytes 393224 | tf_op jit(solution)/shard_map/while/body/eval_jaxpr/ppermute | solution.py:21
  39.2 3.4 collective-permute-done
  52.8 3.5 %collective-permute-start = (bf16[64,1024]{1,0:T(8,128)(2,1)S(1)}, bf16[64,1024]{1,0:T(8,128)(2,1)S(1)}, u32[]{:S(2)}, u32[]{:S(2)}) collective-permute-start(bf16[64,1024]{1,0:T(8,128)(2,1)S(1)} %get-tuple-element.1151), channel_id=1, source_target_pairs={{0,1},{1,2},{2,3},{4,5},{5,6},{6,7},{8,9},{9,10},{10,11},{12,13},{... | collective-permute-start | bytes 393224 | tf_op jit(solution)/shard_map/while/body/eval_jaxpr/ppermute | solution.py:21
  56.3 3.4 collective-permute-done
  69.8 3.5 %collective-permute-start = (bf16[64,1024]{1,0:T(8,128)(2,1)S(1)}, bf16[64,1024]{1,0:T(8,128)(2,1)S(1)}, u32[]{:S(2)}, u32[]{:S(2)}) collective-permute-start(bf16[64,1024]{1,0:T(8,128)(2,1)S(1)} %get-tuple-element.1151), channel_id=1, source_target_pairs={{0,1},{1,2},{2,3},{4,5},{5,6},{6,7},{8,9},{9,10},{10,11},{12,13},{... | collective-permute-start | bytes 393224 | tf_op jit(solution)/shard_map/while/body/eval_jaxpr/ppermute | solution.py:21
  73.3 3.4 collective-permute-done
  86.8 3.5 %collective-permute-start = (bf16[64,1024]{1,0:T(8,128)(2,1)S(1)}, bf16[64,1024]{1,0:T(8,128)(2,1)S(1)}, u32[]{:S(2)}, u32[]{:S(2)}) collective-permute-start(bf16[64,1024]{1,0:T(8,128)(2,1)S(1)} %get-tuple-element.1151), channel_id=1, source_target_pairs={{0,1},{1,2},{2,3},{4,5},{5,6},{6,7},{8,9},{9,10},{10,11},{12,13},{... | collective-permute-start | bytes 393224 | tf_op jit(solution)/shard_map/while/body/eval_jaxpr/ppermute | solution.py:21
  90.3 3.4 collective-permute-done
  93.8 0.8 copy-done.1
  94.7 82.1 %while.58 = (s32[]{:T(128)}, bf16[64,1024]{1,0:T(8,128)(2,1)S(1)}, bf16[2,64,1024]{2,1,0:T(8,128)(2,1)S(1)}, s32[]{:T(128)}, s32[2,2,16]{2,1,0:T(2,128)S(1)}, /*...) while((s32[]{:T(128)}, bf16[64,1024]{1,0:T(8,128)(2,1)S(1)}, ...), condition=%wide.region_3.4_spmd, body=%wide.region_2.3_spmd.sunk | while | flops 299203584 | bytes 19640940 | solution.py:191
  104.3 1.9 collective-permute-start.1
  106.2 4.9 %collective-permute-done.1 = bf16[64,1024]{1,0:T(8,128)(2,1)S(1)} collective-permute-done((bf16[64,1024]{1,0:T(8,128)(2,1)S(1)}, bf16[64,1024]{1,0:T(8,128)(2,1)S(1)}, u32[]{:S(2)}, u32[]{:S(2)}) %collective-permute-start.1) | collective-permute-done | bytes 131104 | tf_op jit(solution)/shard_map/while/body/eval_jaxpr/ppermute | solution.py:21
  120.7 1.9 collective-permute-start.1
  122.7 4.9 %collective-permute-done.1 = bf16[64,1024]{1,0:T(8,128)(2,1)S(1)} collective-permute-done((bf16[64,1024]{1,0:T(8,128)(2,1)S(1)}, bf16[64,1024]{1,0:T(8,128)(2,1)S(1)}, u32[]{:S(2)}, u32[]{:S(2)}) %collective-permute-start.1) | collective-permute-done | bytes 131104 | tf_op jit(solution)/shard_map/while/body/eval_jaxpr/ppermute | solution.py:21
  137.2 1.9 collective-permute-start.1
  139.1 4.9 %collective-permute-done.1 = bf16[64,1024]{1,0:T(8,128)(2,1)S(1)} collective-permute-done((bf16[64,1024]{1,0:T(8,128)(2,1)S(1)}, bf16[64,1024]{1,0:T(8,128)(2,1)S(1)}, u32[]{:S(2)}, u32[]{:S(2)}) %collective-permute-start.1) | collective-permute-done | bytes 131104 | tf_op jit(solution)/shard_map/while/body/eval_jaxpr/ppermute | solution.py:21
  153.6 1.9 collective-permute-start.1
  155.5 4.9 %collective-permute-done.1 = bf16[64,1024]{1,0:T(8,128)(2,1)S(1)} collective-permute-done((bf16[64,1024]{1,0:T(8,128)(2,1)S(1)}, bf16[64,1024]{1,0:T(8,128)(2,1)S(1)}, u32[]{:S(2)}, u32[]{:S(2)}) %collective-permute-start.1) | collective-permute-done | bytes 131104 | tf_op jit(solution)/shard_map/while/body/eval_jaxpr/ppermute | solution.py:21
  170.0 1.9 collective-permute-start.1
  171.9 4.9 %collective-permute-done.1 = bf16[64,1024]{1,0:T(8,128)(2,1)S(1)} collective-permute-done((bf16[64,1024]{1,0:T(8,128)(2,1)S(1)}, bf16[64,1024]{1,0:T(8,128)(2,1)S(1)}, u32[]{:S(2)}, u32[]{:S(2)}) %collective-permute-start.1) | collective-permute-done | bytes 131104 | tf_op jit(solution)/shard_map/while/body/eval_jaxpr/ppermute | solution.py:21
  177.5 22.3 %while.59 = (s32[]{:T(128)}, f32[64,1152]{1,0:T(8,128)S(1)}, f32[48,64]{1,0:T(8,128)S(1)}, f32[]{:T(128)}, bf16[2,48,1024]{2,1,0:T(8,128)(2,1)S(1)}, /*index=5*/...) while((s32[]{:T(128)}, f32[64,1152]{1,0:T(8,128)S(1)}, ...), condition=%wide.region_6.7_spmd.clone, body=%wide.region_4.6_spmd.clone.sunk | while | flops 325101568 | bytes 20380548 | solution.py:205
  182.1 0.8 multiply_reduce_fusion.4
  193.3 0.8 multiply_reduce_fusion.4
  199.9 0.7 copy-done.3
  200.6 40.0 %all-reduce.10 = (f32[48,64]{1,0:T(8,128)S(1)}, f32[]{:T(128)}) all-reduce(f32[48,64]{1,0:T(8,128)S(1)} %get-tuple-element.806, f32[]{:T(128)} %get-tuple-element.807), channel_id=1, replica_groups=mesh['clip'=8,'tm'=4] {'clip','tm'}, use_global_device_ids=true, to_apply=%region_9.10 | all-reduce | flops 3073 | bytes 24584 | tf_op jit(solution)/shard_map/psum | solution.py:207
  241.3 87.1 %all-reduce.13.cloned.1.call-done = f32[64,1152]{1,0:T(8,128)} async-done(((f32[64,1152]{1,0:T(8,128)}), f32[64,1152]{1,0:T(8,128)}) %all-reduce.13.cloned.1.call-update) | async-done | bytes 294928 | tf_op jit(solution)/shard_map/psum | solution.py:207
  328.4 1.7 multiply_reduce_fusion.1
  332.0 0.7 broadcast_multiply_fusion
  (762 shorter events, 117.0 us)
Async XLA Ops:
  7.2 1.0 copy-start.4
  7.2 321.2 %all-reduce.13.cloned.1.call-start = ((), (), s32[]{:S(2)}) async-start(), calls=%async_computation | async-start | bytes 589824 | tf_op jit(solution)/shard_map/psum | solution.py:207
  7.3 0.9 copy-start
  7.3 0.9 copy-start.11
  7.3 0.9 copy-start.13
  7.3 0.9 copy-start.16
  15.3 0.9 copy-start.5
  18.4 7.1 %collective-permute-start = (bf16[64,1024]{1,0:T(8,128)(2,1)S(1)}, bf16[64,1024]{1,0:T(8,128)(2,1)S(1)}, u32[]{:S(2)}, u32[]{:S(2)}) collective-permute-start(bf16[64,1024]{1,0:T(8,128)(2,1)S(1)} %get-tuple-element.1151), channel_id=1, source_target_pairs={{0,1},{1,2},{2,3},{4,5},{5,6},{6,7},{8,9},{9,10},{10,11},{12,13},{... | collective-permute-start | bytes 393224 | tf_op jit(solution)/shard_map/while/body/eval_jaxpr/ppermute | solution.py:21
  32.6 0.9 copy-start.5
  35.7 6.9 %collective-permute-start = (bf16[64,1024]{1,0:T(8,128)(2,1)S(1)}, bf16[64,1024]{1,0:T(8,128)(2,1)S(1)}, u32[]{:S(2)}, u32[]{:S(2)}) collective-permute-start(bf16[64,1024]{1,0:T(8,128)(2,1)S(1)} %get-tuple-element.1151), channel_id=1, source_target_pairs={{0,1},{1,2},{2,3},{4,5},{5,6},{6,7},{8,9},{9,10},{10,11},{12,13},{... | collective-permute-start | bytes 393224 | tf_op jit(solution)/shard_map/while/body/eval_jaxpr/ppermute | solution.py:21
  49.6 0.9 copy-start.5
  52.8 6.9 %collective-permute-start = (bf16[64,1024]{1,0:T(8,128)(2,1)S(1)}, bf16[64,1024]{1,0:T(8,128)(2,1)S(1)}, u32[]{:S(2)}, u32[]{:S(2)}) collective-permute-start(bf16[64,1024]{1,0:T(8,128)(2,1)S(1)} %get-tuple-element.1151), channel_id=1, source_target_pairs={{0,1},{1,2},{2,3},{4,5},{5,6},{6,7},{8,9},{9,10},{10,11},{12,13},{... | collective-permute-start | bytes 393224 | tf_op jit(solution)/shard_map/while/body/eval_jaxpr/ppermute | solution.py:21
  66.7 0.9 copy-start.5
  69.8 6.9 %collective-permute-start = (bf16[64,1024]{1,0:T(8,128)(2,1)S(1)}, bf16[64,1024]{1,0:T(8,128)(2,1)S(1)}, u32[]{:S(2)}, u32[]{:S(2)}) collective-permute-start(bf16[64,1024]{1,0:T(8,128)(2,1)S(1)} %get-tuple-element.1151), channel_id=1, source_target_pairs={{0,1},{1,2},{2,3},{4,5},{5,6},{6,7},{8,9},{9,10},{10,11},{12,13},{... | collective-permute-start | bytes 393224 | tf_op jit(solution)/shard_map/while/body/eval_jaxpr/ppermute | solution.py:21
  83.7 0.9 copy-start.5
  86.8 6.9 %collective-permute-start = (bf16[64,1024]{1,0:T(8,128)(2,1)S(1)}, bf16[64,1024]{1,0:T(8,128)(2,1)S(1)}, u32[]{:S(2)}, u32[]{:S(2)}) collective-permute-start(bf16[64,1024]{1,0:T(8,128)(2,1)S(1)} %get-tuple-element.1151), channel_id=1, source_target_pairs={{0,1},{1,2},{2,3},{4,5},{5,6},{6,7},{8,9},{9,10},{10,11},{12,13},{... | collective-permute-start | bytes 393224 | tf_op jit(solution)/shard_map/while/body/eval_jaxpr/ppermute | solution.py:21
  93.7 0.9 copy-start.1
  93.7 1.0 copy-start.6
  93.7 0.9 copy-start.12
  93.7 0.9 copy-start.14
  93.8 0.9 copy-start.17
  94.7 82.2 %copy-start.2 = (bf16[64,1152]{1,0:T(8,128)(2,1)S(1)}, bf16[64,1152]{1,0:T(8,128)(2,1)}, u32[]{:S(2)}) copy-start(bf16[64,1152]{1,0:T(8,128)(2,1)} %param.33) | copy-start | bytes 442372
  94.7 82.2 %copy-start.7 = (bf16[2,1,48,1024]{3,2,1,0:T(8,128)(2,1)S(1)}, bf16[2,1,48,1024]{3,2,1,0:T(8,128)(2,1)}, u32[]{:S(2)}) copy-start(bf16[2,1,48,1024]{3,2,1,0:T(8,128)(2,1)} %param.37) | copy-start | bytes 589828
  94.7 82.2 %copy-start.9 = (bf16[48,64]{1,0:T(8,128)(2,1)S(1)}, bf16[48,64]{1,0:T(8,128)(2,1)}, u32[]{:S(2)}) copy-start(bf16[48,64]{1,0:T(8,128)(2,1)} %param.35) | copy-start | bytes 18436
  104.3 6.9 %collective-permute-start.1 = (bf16[64,1024]{1,0:T(8,128)(2,1)S(1)}, bf16[64,1024]{1,0:T(8,128)(2,1)S(1)}, u32[]{:S(2)}, u32[]{:S(2)}) collective-permute-start(bf16[64,1024]{1,0:T(8,128)(2,1)S(1)} %get-tuple-element.1171), channel_id=1, source_target_pairs={{1,0},{2,1},{3,2},{5,4},{6,5},{7,6},{9,8},{10,9},{11,10},{13,12},{... | collective-permute-start | bytes 393224 | tf_op jit(solution)/shard_map/while/body/eval_jaxpr/ppermute | solution.py:21
  120.7 6.9 %collective-permute-start.1 = (bf16[64,1024]{1,0:T(8,128)(2,1)S(1)}, bf16[64,1024]{1,0:T(8,128)(2,1)S(1)}, u32[]{:S(2)}, u32[]{:S(2)}) collective-permute-start(bf16[64,1024]{1,0:T(8,128)(2,1)S(1)} %get-tuple-element.1171), channel_id=1, source_target_pairs={{1,0},{2,1},{3,2},{5,4},{6,5},{7,6},{9,8},{10,9},{11,10},{13,12},{... | collective-permute-start | bytes 393224 | tf_op jit(solution)/shard_map/while/body/eval_jaxpr/ppermute | solution.py:21
  137.2 6.9 %collective-permute-start.1 = (bf16[64,1024]{1,0:T(8,128)(2,1)S(1)}, bf16[64,1024]{1,0:T(8,128)(2,1)S(1)}, u32[]{:S(2)}, u32[]{:S(2)}) collective-permute-start(bf16[64,1024]{1,0:T(8,128)(2,1)S(1)} %get-tuple-element.1171), channel_id=1, source_target_pairs={{1,0},{2,1},{3,2},{5,4},{6,5},{7,6},{9,8},{10,9},{11,10},{13,12},{... | collective-permute-start | bytes 393224 | tf_op jit(solution)/shard_map/while/body/eval_jaxpr/ppermute | solution.py:21
  153.6 6.9 %collective-permute-start.1 = (bf16[64,1024]{1,0:T(8,128)(2,1)S(1)}, bf16[64,1024]{1,0:T(8,128)(2,1)S(1)}, u32[]{:S(2)}, u32[]{:S(2)}) collective-permute-start(bf16[64,1024]{1,0:T(8,128)(2,1)S(1)} %get-tuple-element.1171), channel_id=1, source_target_pairs={{1,0},{2,1},{3,2},{5,4},{6,5},{7,6},{9,8},{10,9},{11,10},{13,12},{... | collective-permute-start | bytes 393224 | tf_op jit(solution)/shard_map/while/body/eval_jaxpr/ppermute | solution.py:21
  170.0 6.9 %collective-permute-start.1 = (bf16[64,1024]{1,0:T(8,128)(2,1)S(1)}, bf16[64,1024]{1,0:T(8,128)(2,1)S(1)}, u32[]{:S(2)}, u32[]{:S(2)}) collective-permute-start(bf16[64,1024]{1,0:T(8,128)(2,1)S(1)} %get-tuple-element.1171), channel_id=1, source_target_pairs={{1,0},{2,1},{3,2},{5,4},{6,5},{7,6},{9,8},{10,9},{11,10},{13,12},{... | collective-permute-start | bytes 393224 | tf_op jit(solution)/shard_map/while/body/eval_jaxpr/ppermute | solution.py:21
  199.9 0.7 copy-start.3
  199.9 130.2 %copy-start.15 = (bf16[2,48,1024]{2,1,0:T(8,128)(2,1)}, bf16[2,48,1024]{2,1,0:T(8,128)(2,1)S(1)}, u32[]{:S(2)}) copy-start(bf16[2,48,1024]{2,1,0:T(8,128)(2,1)S(1)} %get-tuple-element.804) | copy-start | bytes 589828
  328.4 3.6 %copy-start.8 = (f32[64,1152]{1,0:T(8,128)S(1)}, f32[64,1152]{1,0:T(8,128)}, u32[]{:S(2)}) copy-start(f32[64,1152]{1,0:T(8,128)} %all-reduce.13.cloned.1.call-done) | copy-start | bytes 884740
  (2 other events, 1.3 us)
Sparse Core Ops, SparseCore 0:
  200.7 127.6 all-reduce.12
where the time goes:
time: 340 us
  waiting for transfers between devices  129 us (38%)
  matrix products  94.4 us (28%)
  blocking collectives  40 us (12%)
  starting transfers between devices  27.1 us (8%)
  local copies, waits for them, and re-layouts  23.4 us (7%)
  between operations  15.5 us (5%)
  other arithmetic  5.51 us (2%)
  loops' own time  4.82 us (1%)
    psum x1, waiting for transfers between devices, on_device(): lax.psum((totals[0], totals[1], totals[2]), ('clip', 'tm'))  87.1 us
    dot_general x306, matrix products, apply_taps(): term = jnp.dot(block, group[tap_index], preferred_element_type=jnp.float32)  74 us
    ppermute x10, waiting for transfers between devices, shifted(): lax.ppermute(value, axis, [(source, source + steps) for source in range(f...  41.7 us
    psum x1, blocking collectives, on_device(): lax.psum((totals[0], totals[1], totals[2]), ('clip', 'tm'))  40 us
    ppermute x10, starting transfers between devices, shifted(): lax.ppermute(value, axis, [(source, source + steps) for source in range(f...  27.1 us
    dot_general x40, matrix products, warp_state(): pieces.append(jnp.dot(window, one_hot, preferred_element_type=jnp.float32))  9.38 us
    dot_general x36, matrix products, merge_and_grade(): lax.dot_general(d_mixed, group[tap_index], (((1,), (1,)), ((), ())), pref...  8.63 us
  transfers between devices with their start and end apart: 11, of which 11 were waited for; matrix products, arithmetic and copies ran while one was open for 0% of the time, Pallas kernels for 0%

commit v1 on v0

--- a/solution.py
+++ b/solution.py
@@ -1,3 +1,4 @@
+import functools
 import jax
 import jax.numpy as jnp
 from jax import lax
@@ -13,6 +14,13 @@
 block_side = 8
 clip_limit = 128.0
 leak_slope = 0.1
+
+
+def lane_load(block_here, link_axis, named_axis):
+    return lax.psum(lax.psum(block_here, named_axis), link_axis)
+
+
+outputs_switch = functools.partial(lane_load, link_axis="clip", named_axis="tm")
 
 
 def shifted(value, axis, steps):
@@ -204,7 +212,7 @@
     )
     totals, frames_out = lax.scan(grade_member, initial, (fwd_states, bwd_states, target[:, 0]))
     restored = frames_out[:, None]
-    grad_merge, grad_head, loss_total = lax.psum((totals[0], totals[1], totals[2]), ("clip", "tm"))
+    grad_merge, grad_head, loss_total = outputs_switch((totals[0], totals[1], totals[2]))
     squares = jnp.sum(grad_merge * grad_merge) + jnp.sum(grad_head * grad_head)
     factor = jnp.minimum(1.0, clip_limit / jnp.sqrt(squares + 1e-06))
     return (restored, grad_merge * factor, grad_head * factor, loss_total)

time: 340 us -> 306 us (0.900)
  waiting for transfers between devices: 129 us -> 94.6 us
    psum x1 -> x2, waiting for transfers between devices: 87.1 us -> 52.8 us  [lane_load(): return lax.psum(lax.psum(block_here, named_axis), link_axis)]
    psum x1 -> x2, blocking collectives: 40 us -> 38.5 us  [lane_load(): return lax.psum(lax.psum(block_here, named_axis), link_axis)]
  transfers between devices with their start and end apart: 11 -> 12, of which waited for: 11 -> 12; matrix products, arithmetic and copies ran while one was open for 0% -> 0% of each run, Pallas kernels for 0% -> 0%
where the time goes in v1:
time: 306 us; the launch traced here: 304 us
  waiting for transfers between devices  94.6 us (31%)
  matrix products  94.4 us (31%)
  blocking collectives  38.5 us (13%)
  starting transfers between devices  27.1 us (9%)
  local copies, waits for them, and re-layouts  23.4 us (8%)
  between operations  15.6 us (5%)
  other arithmetic  5.48 us (2%)
  loops' own time  4.83 us (2%)
    dot_general x306, matrix products, apply_taps(): term = jnp.dot(block, group[tap_index], preferred_element_type=jnp.float32)  74 us
    psum x2, waiting for transfers between devices, lane_load(): return lax.psum(lax.psum(block_here, named_axis), link_axis)  52.8 us
    ppermute x10, waiting for transfers between devices, shifted(): lax.ppermute(value, axis, [(source, source + steps) for source in range(f...  41.7 us
    psum x2, blocking collectives, lane_load(): return lax.psum(lax.psum(block_here, named_axis), link_axis)  38.5 us
    ppermute x10, starting transfers between devices, shifted(): lax.ppermute(value, axis, [(source, source + steps) for source in range(f...  27.1 us
    dot_general x40, matrix products, warp_state(): pieces.append(jnp.dot(window, one_hot, preferred_element_type=jnp.float32))  9.38 us
    dot_general x36, matrix products, merge_and_grade(): lax.dot_general(d_mixed, group[tap_index], (((1,), (1,)), ((), ())), pref...  8.61 us
    broadcast_in_dim x80, local copies, waits for them, and re-layouts, warp_state(): jnp.repeat(jnp.repeat(flow_map[0].reshape(grid_shape), block_side, 0), bl...  6.18 us
  transfers between devices with their start and end apart: 12, of which 12 were waited for; matrix products, arithmetic and copies ran while one was open for 0% of the time, Pallas kernels for 0%

profile of v1, /device:TPU:8, one launch (start us, length us, event | category | flops | bytes accessed | tf_op | source)
XLA Modules:
  0.0 303.9 jit_solution(6906959869907186397)
XLA Ops:
  7.4 0.8 copy-done.4
  8.2 85.5 %while.57 = (s32[]{:T(128)}, bf16[64,1024]{1,0:T(8,128)(2,1)S(1)}, bf16[2,64,1024]{2,1,0:T(8,128)(2,1)S(1)}, s32[]{:T(128)}, s32[2,2,16]{2,1,0:T(2,128)S(1)}, /*...) while((s32[]{:T(128)}, bf16[64,1024]{1,0:T(8,128)(2,1)S(1)}, ...), condition=%wide.region_1.2_spmd, body=%wide.region_0.1_spmd.sunk | while | flops 299203584 | bytes 19935880 | solution.py:198
  18.4 3.5 %collective-permute-start = (bf16[64,1024]{1,0:T(8,128)(2,1)S(1)}, bf16[64,1024]{1,0:T(8,128)(2,1)S(1)}, u32[]{:S(2)}, u32[]{:S(2)}) collective-permute-start(bf16[64,1024]{1,0:T(8,128)(2,1)S(1)} %get-tuple-element.1153), channel_id=1, source_target_pairs={{0,1},{1,2},{2,3},{4,5},{5,6},{6,7},{8,9},{9,10},{10,11},{12,13},{... | collective-permute-start | bytes 393224 | tf_op jit(solution)/shard_map/while/body/eval_jaxpr/ppermute | solution.py:29
  21.9 3.6 %collective-permute-done = bf16[64,1024]{1,0:T(8,128)(2,1)S(1)} collective-permute-done((bf16[64,1024]{1,0:T(8,128)(2,1)S(1)}, bf16[64,1024]{1,0:T(8,128)(2,1)S(1)}, u32[]{:S(2)}, u32[]{:S(2)}) %collective-permute-start) | collective-permute-done | bytes 131104 | tf_op jit(solution)/shard_map/while/body/eval_jaxpr/ppermute | solution.py:29
  35.7 3.5 %collective-permute-start = (bf16[64,1024]{1,0:T(8,128)(2,1)S(1)}, bf16[64,1024]{1,0:T(8,128)(2,1)S(1)}, u32[]{:S(2)}, u32[]{:S(2)}) collective-permute-start(bf16[64,1024]{1,0:T(8,128)(2,1)S(1)} %get-tuple-element.1153), channel_id=1, source_target_pairs={{0,1},{1,2},{2,3},{4,5},{5,6},{6,7},{8,9},{9,10},{10,11},{12,13},{... | collective-permute-start | bytes 393224 | tf_op jit(solution)/shard_map/while/body/eval_jaxpr/ppermute | solution.py:29
  39.2 3.4 %collective-permute-done = bf16[64,1024]{1,0:T(8,128)(2,1)S(1)} collective-permute-done((bf16[64,1024]{1,0:T(8,128)(2,1)S(1)}, bf16[64,1024]{1,0:T(8,128)(2,1)S(1)}, u32[]{:S(2)}, u32[]{:S(2)}) %collective-permute-start) | collective-permute-done | bytes 131104 | tf_op jit(solution)/shard_map/while/body/eval_jaxpr/ppermute | solution.py:29
  52.8 3.5 %collective-permute-start = (bf16[64,1024]{1,0:T(8,128)(2,1)S(1)}, bf16[64,1024]{1,0:T(8,128)(2,1)S(1)}, u32[]{:S(2)}, u32[]{:S(2)}) collective-permute-start(bf16[64,1024]{1,0:T(8,128)(2,1)S(1)} %get-tuple-element.1153), channel_id=1, source_target_pairs={{0,1},{1,2},{2,3},{4,5},{5,6},{6,7},{8,9},{9,10},{10,11},{12,13},{... | collective-permute-start | bytes 393224 | tf_op jit(solution)/shard_map/while/body/eval_jaxpr/ppermute | solution.py:29
  56.3 3.4 %collective-permute-done = bf16[64,1024]{1,0:T(8,128)(2,1)S(1)} collective-permute-done((bf16[64,1024]{1,0:T(8,128)(2,1)S(1)}, bf16[64,1024]{1,0:T(8,128)(2,1)S(1)}, u32[]{:S(2)}, u32[]{:S(2)}) %collective-permute-start) | collective-permute-done | bytes 131104 | tf_op jit(solution)/shard_map/while/body/eval_jaxpr/ppermute | solution.py:29
  69.8 3.5 %collective-permute-start = (bf16[64,1024]{1,0:T(8,128)(2,1)S(1)}, bf16[64,1024]{1,0:T(8,128)(2,1)S(1)}, u32[]{:S(2)}, u32[]{:S(2)}) collective-permute-start(bf16[64,1024]{1,0:T(8,128)(2,1)S(1)} %get-tuple-element.1153), channel_id=1, source_target_pairs={{0,1},{1,2},{2,3},{4,5},{5,6},{6,7},{8,9},{9,10},{10,11},{12,13},{... | collective-permute-start | bytes 393224 | tf_op jit(solution)/shard_map/while/body/eval_jaxpr/ppermute | solution.py:29
  73.3 3.4 %collective-permute-done = bf16[64,1024]{1,0:T(8,128)(2,1)S(1)} collective-permute-done((bf16[64,1024]{1,0:T(8,128)(2,1)S(1)}, bf16[64,1024]{1,0:T(8,128)(2,1)S(1)}, u32[]{:S(2)}, u32[]{:S(2)}) %collective-permute-start) | collective-permute-done | bytes 131104 | tf_op jit(solution)/shard_map/while/body/eval_jaxpr/ppermute | solution.py:29
  86.8 3.5 %collective-permute-start = (bf16[64,1024]{1,0:T(8,128)(2,1)S(1)}, bf16[64,1024]{1,0:T(8,128)(2,1)S(1)}, u32[]{:S(2)}, u32[]{:S(2)}) collective-permute-start(bf16[64,1024]{1,0:T(8,128)(2,1)S(1)} %get-tuple-element.1153), channel_id=1, source_target_pairs={{0,1},{1,2},{2,3},{4,5},{5,6},{6,7},{8,9},{9,10},{10,11},{12,13},{... | collective-permute-start | bytes 393224 | tf_op jit(solution)/shard_map/while/body/eval_jaxpr/ppermute | solution.py:29
  90.3 3.4 %collective-permute-done = bf16[64,1024]{1,0:T(8,128)(2,1)S(1)} collective-permute-done((bf16[64,1024]{1,0:T(8,128)(2,1)S(1)}, bf16[64,1024]{1,0:T(8,128)(2,1)S(1)}, u32[]{:S(2)}, u32[]{:S(2)}) %collective-permute-start) | collective-permute-done | bytes 131104 | tf_op jit(solution)/shard_map/while/body/eval_jaxpr/ppermute | solution.py:29
  93.8 0.8 copy-done.1
  94.7 82.1 %while.58 = (s32[]{:T(128)}, bf16[64,1024]{1,0:T(8,128)(2,1)S(1)}, bf16[2,64,1024]{2,1,0:T(8,128)(2,1)S(1)}, s32[]{:T(128)}, s32[2,2,16]{2,1,0:T(2,128)S(1)}, /*...) while((s32[]{:T(128)}, bf16[64,1024]{1,0:T(8,128)(2,1)S(1)}, ...), condition=%wide.region_3.4_spmd, body=%wide.region_2.3_spmd.sunk | while | flops 299203584 | bytes 19640940 | solution.py:199
  104.3 1.9 collective-permute-start.1
  106.2 4.9 %collective-permute-done.1 = bf16[64,1024]{1,0:T(8,128)(2,1)S(1)} collective-permute-done((bf16[64,1024]{1,0:T(8,128)(2,1)S(1)}, bf16[64,1024]{1,0:T(8,128)(2,1)S(1)}, u32[]{:S(2)}, u32[]{:S(2)}) %collective-permute-start.1) | collective-permute-done | bytes 131104 | tf_op jit(solution)/shard_map/while/body/eval_jaxpr/ppermute | solution.py:29
  120.7 1.9 collective-permute-start.1
  122.7 4.9 %collective-permute-done.1 = bf16[64,1024]{1,0:T(8,128)(2,1)S(1)} collective-permute-done((bf16[64,1024]{1,0:T(8,128)(2,1)S(1)}, bf16[64,1024]{1,0:T(8,128)(2,1)S(1)}, u32[]{:S(2)}, u32[]{:S(2)}) %collective-permute-start.1) | collective-permute-done | bytes 131104 | tf_op jit(solution)/shard_map/while/body/eval_jaxpr/ppermute | solution.py:29
  137.2 1.9 collective-permute-start.1
  139.1 4.9 %collective-permute-done.1 = bf16[64,1024]{1,0:T(8,128)(2,1)S(1)} collective-permute-done((bf16[64,1024]{1,0:T(8,128)(2,1)S(1)}, bf16[64,1024]{1,0:T(8,128)(2,1)S(1)}, u32[]{:S(2)}, u32[]{:S(2)}) %collective-permute-start.1) | collective-permute-done | bytes 131104 | tf_op jit(solution)/shard_map/while/body/eval_jaxpr/ppermute | solution.py:29
  153.6 1.9 collective-permute-start.1
  155.5 4.9 %collective-permute-done.1 = bf16[64,1024]{1,0:T(8,128)(2,1)S(1)} collective-permute-done((bf16[64,1024]{1,0:T(8,128)(2,1)S(1)}, bf16[64,1024]{1,0:T(8,128)(2,1)S(1)}, u32[]{:S(2)}, u32[]{:S(2)}) %collective-permute-start.1) | collective-permute-done | bytes 131104 | tf_op jit(solution)/shard_map/while/body/eval_jaxpr/ppermute | solution.py:29
  170.0 1.9 collective-permute-start.1
  171.9 4.9 %collective-permute-done.1 = bf16[64,1024]{1,0:T(8,128)(2,1)S(1)} collective-permute-done((bf16[64,1024]{1,0:T(8,128)(2,1)S(1)}, bf16[64,1024]{1,0:T(8,128)(2,1)S(1)}, u32[]{:S(2)}, u32[]{:S(2)}) %collective-permute-start.1) | collective-permute-done | bytes 131104 | tf_op jit(solution)/shard_map/while/body/eval_jaxpr/ppermute | solution.py:29
  177.5 22.3 %while.59 = (s32[]{:T(128)}, f32[64,1152]{1,0:T(8,128)S(1)}, f32[48,64]{1,0:T(8,128)S(1)}, f32[]{:T(128)}, bf16[2,48,1024]{2,1,0:T(8,128)(2,1)S(1)}, /*index=5*/...) while((s32[]{:T(128)}, f32[64,1152]{1,0:T(8,128)S(1)}, ...), condition=%wide.region_6.7_spmd.clone, body=%wide.region_4.6_spmd.clone.sunk | while | flops 325101568 | bytes 20380548 | solution.py:213
  182.1 0.8 multiply_reduce_fusion.4
  193.3 0.8 multiply_reduce_fusion.4
  200.7 35.9 %all-reduce.15.cloned.1.call-done = f32[64,1152]{1,0:T(8,128)} async-done(((f32[64,1152]{1,0:T(8,128)}), f32[64,1152]{1,0:T(8,128)}) %all-reduce.15.cloned.1.call-update) | async-done | bytes 294928 | tf_op jit(solution)/shard_map/psum | solution.py:20
  236.6 16.0 %all-reduce.11 = (f32[48,64]{1,0:T(8,128)S(1)}, f32[]{:T(128)}) all-reduce(f32[48,64]{1,0:T(8,128)S(1)} %get-tuple-element.806, f32[]{:T(128)} %get-tuple-element.807), channel_id=1, replica_groups=mesh['clip'=8,'tm'=4] {'tm'}, use_global_device_ids=true, to_apply=%region_10.11 | all-reduce | flops 3073 | bytes 24584 | tf_op jit(solution)/shard_map/psum | solution.py:20
  252.6 22.4 %all-reduce.10 = (f32[48,64]{1,0:T(8,128)S(1)}, f32[]{:T(128)}) all-reduce(f32[48,64]{1,0:T(8,128)S(1)} %get-tuple-element.913, f32[]{:T(128)} %get-tuple-element.914), channel_id=1, replica_groups=mesh['clip'=8,'tm'=4] {'clip'}, use_global_device_ids=true, to_apply=%region_11.12 | all-reduce | flops 3073 | bytes 24584 | tf_op jit(solution)/shard_map/psum | solution.py:20
  275.7 16.9 %all-reduce.17.cloned.1.call-done = f32[64,1152]{1,0:T(8,128)} async-done(((f32[64,1152]{1,0:T(8,128)}), f32[64,1152]{1,0:T(8,128)}) %all-reduce.17.cloned.1.call-update) | async-done | bytes 294928 | tf_op jit(solution)/shard_map/psum | solution.py:20
  292.6 1.7 multiply_reduce_fusion.1
  (766 shorter events, 118.5 us)
Async XLA Ops:
  7.2 1.0 copy-start.4
  7.2 229.4 %all-reduce.15.cloned.1.call-start = ((), (), s32[]{:S(2)}) async-start(), calls=%async_computation | async-start | bytes 589824 | tf_op jit(solution)/shard_map/psum | solution.py:20
  7.3 0.9 copy-start
  7.3 0.9 copy-start.11
  7.3 0.9 copy-start.13
  7.3 0.9 copy-start.16
  15.3 0.9 copy-start.5
  18.4 7.1 %collective-permute-start = (bf16[64,1024]{1,0:T(8,128)(2,1)S(1)}, bf16[64,1024]{1,0:T(8,128)(2,1)S(1)}, u32[]{:S(2)}, u32[]{:S(2)}) collective-permute-start(bf16[64,1024]{1,0:T(8,128)(2,1)S(1)} %get-tuple-element.1153), channel_id=1, source_target_pairs={{0,1},{1,2},{2,3},{4,5},{5,6},{6,7},{8,9},{9,10},{10,11},{12,13},{... | collective-permute-start | bytes 393224 | tf_op jit(solution)/shard_map/while/body/eval_jaxpr/ppermute | solution.py:29
  32.6 0.9 copy-start.5
  35.7 6.9 %collective-permute-start = (bf16[64,1024]{1,0:T(8,128)(2,1)S(1)}, bf16[64,1024]{1,0:T(8,128)(2,1)S(1)}, u32[]{:S(2)}, u32[]{:S(2)}) collective-permute-start(bf16[64,1024]{1,0:T(8,128)(2,1)S(1)} %get-tuple-element.1153), channel_id=1, source_target_pairs={{0,1},{1,2},{2,3},{4,5},{5,6},{6,7},{8,9},{9,10},{10,11},{12,13},{... | collective-permute-start | bytes 393224 | tf_op jit(solution)/shard_map/while/body/eval_jaxpr/ppermute | solution.py:29
  49.6 0.9 copy-start.5
  52.8 6.9 %collective-permute-start = (bf16[64,1024]{1,0:T(8,128)(2,1)S(1)}, bf16[64,1024]{1,0:T(8,128)(2,1)S(1)}, u32[]{:S(2)}, u32[]{:S(2)}) collective-permute-start(bf16[64,1024]{1,0:T(8,128)(2,1)S(1)} %get-tuple-element.1153), channel_id=1, source_target_pairs={{0,1},{1,2},{2,3},{4,5},{5,6},{6,7},{8,9},{9,10},{10,11},{12,13},{... | collective-permute-start | bytes 393224 | tf_op jit(solution)/shard_map/while/body/eval_jaxpr/ppermute | solution.py:29
  66.7 0.9 copy-start.5
  69.8 6.9 %collective-permute-start = (bf16[64,1024]{1,0:T(8,128)(2,1)S(1)}, bf16[64,1024]{1,0:T(8,128)(2,1)S(1)}, u32[]{:S(2)}, u32[]{:S(2)}) collective-permute-start(bf16[64,1024]{1,0:T(8,128)(2,1)S(1)} %get-tuple-element.1153), channel_id=1, source_target_pairs={{0,1},{1,2},{2,3},{4,5},{5,6},{6,7},{8,9},{9,10},{10,11},{12,13},{... | collective-permute-start | bytes 393224 | tf_op jit(solution)/shard_map/while/body/eval_jaxpr/ppermute | solution.py:29
  83.7 0.9 copy-start.5
  86.8 6.9 %collective-permute-start = (bf16[64,1024]{1,0:T(8,128)(2,1)S(1)}, bf16[64,1024]{1,0:T(8,128)(2,1)S(1)}, u32[]{:S(2)}, u32[]{:S(2)}) collective-permute-start(bf16[64,1024]{1,0:T(8,128)(2,1)S(1)} %get-tuple-element.1153), channel_id=1, source_target_pairs={{0,1},{1,2},{2,3},{4,5},{5,6},{6,7},{8,9},{9,10},{10,11},{12,13},{... | collective-permute-start | bytes 393224 | tf_op jit(solution)/shard_map/while/body/eval_jaxpr/ppermute | solution.py:29
  93.7 0.9 copy-start.1
  93.7 1.0 copy-start.6
  93.7 0.9 copy-start.12
  93.7 0.9 copy-start.14
  93.8 0.9 copy-start.17
  94.7 82.2 %copy-start.2 = (bf16[64,1152]{1,0:T(8,128)(2,1)S(1)}, bf16[64,1152]{1,0:T(8,128)(2,1)}, u32[]{:S(2)}) copy-start(bf16[64,1152]{1,0:T(8,128)(2,1)} %param.33) | copy-start | bytes 442372
  94.7 82.2 %copy-start.7 = (bf16[2,1,48,1024]{3,2,1,0:T(8,128)(2,1)S(1)}, bf16[2,1,48,1024]{3,2,1,0:T(8,128)(2,1)}, u32[]{:S(2)}) copy-start(bf16[2,1,48,1024]{3,2,1,0:T(8,128)(2,1)} %param.37) | copy-start | bytes 589828
  94.7 82.2 %copy-start.9 = (bf16[48,64]{1,0:T(8,128)(2,1)S(1)}, bf16[48,64]{1,0:T(8,128)(2,1)}, u32[]{:S(2)}) copy-start(bf16[48,64]{1,0:T(8,128)(2,1)} %param.35) | copy-start | bytes 18436
  104.3 6.9 %collective-permute-start.1 = (bf16[64,1024]{1,0:T(8,128)(2,1)S(1)}, bf16[64,1024]{1,0:T(8,128)(2,1)S(1)}, u32[]{:S(2)}, u32[]{:S(2)}) collective-permute-start(bf16[64,1024]{1,0:T(8,128)(2,1)S(1)} %get-tuple-element.1173), channel_id=1, source_target_pairs={{1,0},{2,1},{3,2},{5,4},{6,5},{7,6},{9,8},{10,9},{11,10},{13,12},{... | collective-permute-start | bytes 393224 | tf_op jit(solution)/shard_map/while/body/eval_jaxpr/ppermute | solution.py:29
  120.7 6.9 %collective-permute-start.1 = (bf16[64,1024]{1,0:T(8,128)(2,1)S(1)}, bf16[64,1024]{1,0:T(8,128)(2,1)S(1)}, u32[]{:S(2)}, u32[]{:S(2)}) collective-permute-start(bf16[64,1024]{1,0:T(8,128)(2,1)S(1)} %get-tuple-element.1173), channel_id=1, source_target_pairs={{1,0},{2,1},{3,2},{5,4},{6,5},{7,6},{9,8},{10,9},{11,10},{13,12},{... | collective-permute-start | bytes 393224 | tf_op jit(solution)/shard_map/while/body/eval_jaxpr/ppermute | solution.py:29
  137.2 6.9 %collective-permute-start.1 = (bf16[64,1024]{1,0:T(8,128)(2,1)S(1)}, bf16[64,1024]{1,0:T(8,128)(2,1)S(1)}, u32[]{:S(2)}, u32[]{:S(2)}) collective-permute-start(bf16[64,1024]{1,0:T(8,128)(2,1)S(1)} %get-tuple-element.1173), channel_id=1, source_target_pairs={{1,0},{2,1},{3,2},{5,4},{6,5},{7,6},{9,8},{10,9},{11,10},{13,12},{... | collective-permute-start | bytes 393224 | tf_op jit(solution)/shard_map/while/body/eval_jaxpr/ppermute | solution.py:29
  153.6 6.9 %collective-permute-start.1 = (bf16[64,1024]{1,0:T(8,128)(2,1)S(1)}, bf16[64,1024]{1,0:T(8,128)(2,1)S(1)}, u32[]{:S(2)}, u32[]{:S(2)}) collective-permute-start(bf16[64,1024]{1,0:T(8,128)(2,1)S(1)} %get-tuple-element.1173), channel_id=1, source_target_pairs={{1,0},{2,1},{3,2},{5,4},{6,5},{7,6},{9,8},{10,9},{11,10},{13,12},{... | collective-permute-start | bytes 393224 | tf_op jit(solution)/shard_map/while/body/eval_jaxpr/ppermute | solution.py:29
  170.0 6.9 %collective-permute-start.1 = (bf16[64,1024]{1,0:T(8,128)(2,1)S(1)}, bf16[64,1024]{1,0:T(8,128)(2,1)S(1)}, u32[]{:S(2)}, u32[]{:S(2)}) collective-permute-start(bf16[64,1024]{1,0:T(8,128)(2,1)S(1)} %get-tuple-element.1173), channel_id=1, source_target_pairs={{1,0},{2,1},{3,2},{5,4},{6,5},{7,6},{9,8},{10,9},{11,10},{13,12},{... | collective-permute-start | bytes 393224 | tf_op jit(solution)/shard_map/while/body/eval_jaxpr/ppermute | solution.py:29
  199.9 36.7 %copy-start.15 = (bf16[2,48,1024]{2,1,0:T(8,128)(2,1)}, bf16[2,48,1024]{2,1,0:T(8,128)(2,1)S(1)}, u32[]{:S(2)}) copy-start(bf16[2,48,1024]{2,1,0:T(8,128)(2,1)S(1)} %get-tuple-element.804) | copy-start | bytes 589828
  200.6 92.0 %all-reduce.17.cloned.1.call-start = ((), (), s32[]{:S(2)}) async-start(), calls=%async_computation.1 | async-start | bytes 589824 | tf_op jit(solution)/shard_map/psum | solution.py:20
  292.6 3.7 %copy-start.8 = (f32[64,1152]{1,0:T(8,128)S(1)}, f32[64,1152]{1,0:T(8,128)}, u32[]{:S(2)}) copy-start(f32[64,1152]{1,0:T(8,128)} %all-reduce.17.cloned.1.call-done) | copy-start | bytes 884740
  (3 other events, 2.0 us)
Sparse Core Ops, SparseCore 0:
  200.7 35.8 all-reduce.14
  239.7 52.8 all-reduce.16
